TPU v7x, 256 devices: a whole 4x4x8 slice. The times are simulated.
256 devices in a mesh: pb: 16 (over x, z_hi), sa: 16 (over z_lo, y, core).
Axes of the slice: x: 4, y: 4, z: 8 (z_hi: 4, z_lo: 2; z = z_hi * 2 + z_lo), core: 2. Of those that a mesh axis runs over, the one named last changes fastest.
Arguments:
- question_states: bfloat16 [16, 16, 256, 768], P('pb', 'sa'), may hold values from -16 to 16
- question_ids: int32 [16, 16, 256], P('pb'), may hold values from 0 to 30521, as said below
- q_inner_weight: bfloat16 [768, 3072], P(None, 'sa'), may hold values from -0.21875 to 0.21875
- q_outer_weight: bfloat16 [3072, 768], P('sa'), may hold values from -0.109375 to 0.109375
- q_norm_gain: float32 [768], replicated, may hold values from 0.1 to 1.9
- sql_states: bfloat16 [16, 16, 256, 768], P('sa', 'pb'), may hold values from -16 to 16
- sql_ids: int32 [16, 16, 256], P('sa'), may hold values from 0 to 32099, as said below
- s_inner_weight: bfloat16 [768, 3072], P(None, 'pb'), may hold values from -0.21875 to 0.21875
- s_outer_weight: bfloat16 [3072, 768], P('pb'), may hold values from -0.109375 to 0.109375
- s_norm_gain: float32 [768], replicated, may hold values from 0.1 to 1.9
- positive_column: int32 [256], P('pb'), may hold values from 0 to 255, each once
Outputs:
- loss: float32 [], replicated
- q_inner_grad: float32 [768, 3072], P(None, 'sa')
- q_outer_grad: float32 [3072, 768], P('sa')
- q_gain_grad: float32 [768], replicated
- s_inner_grad: float32 [768, 3072], P(None, 'pb')
- s_outer_grad: float32 [3072, 768], P('pb')
- s_gain_grad: float32 [768], replicated
Inputs may be any that keep to these rules, and one draw needn't show every extreme that they name: `question_ids`: each sequence is a run of nonzero ids followed by padding zeros, the run 3 * 64 long or longer. `sql_ids`: each sequence is a run of nonzero ids followed by padding zeros, the run 3 * 64 long or longer.
All inputs are finite; a program needn't handle non-finite values.
Results may differ from a plain program's by a relative error of at most 0.0051.
Values may be sent and summed in bfloat16 or wider, within the bound.
A program may use at most 128 MiB of HBM per device.

v0:
```python
import math

import jax
import jax.numpy as jnp
from jax import lax
from jax.sharding import PartitionSpec as P

D = 768


HIGH = lax.Precision.HIGHEST


def apply_rms_norm(input_float, norm_gain_vector, root_mean_square):
    if root_mean_square:
        input_normalized = input_float * lax.rsqrt(
            jnp.mean(input_float * input_float, axis=-1, keepdims=True) + 1e-06
        )
    else:
        mean_removed = input_float - jnp.mean(input_float, axis=-1, keepdims=True)
        input_normalized = mean_removed * lax.rsqrt(
            jnp.mean(mean_removed * mean_removed, axis=-1, keepdims=True) + 1e-05
        )
    return (input_normalized, (input_normalized * norm_gain_vector).astype(jnp.bfloat16))


def gelu_value(v):
    return 0.5 * v * (1.0 + lax.erf(v / math.sqrt(2.0)))


def gelu_slope(v):
    return 0.5 * (1.0 + lax.erf(v / math.sqrt(2.0))) + v * jnp.exp(-0.5 * v * v) / math.sqrt(
        2.0 * math.pi
    )


def pool_weights(ids):
    mask = (ids > 0).astype(jnp.float32)
    return mask / jnp.sum(mask, axis=-1, keepdims=True)


def forward_block(states, ids, inner, norm_gain_vector, root_mean_square):
    count, length, width = states.shape
    input_float = states.astype(jnp.float32).reshape(count * length, width)
    input_normalized, normalized_rows = apply_rms_norm(
        input_float, norm_gain_vector, root_mean_square
    )
    pre = jnp.dot(normalized_rows, inner, preferred_element_type=jnp.float32)
    hidden = gelu_value(pre).reshape(count, length, -1)
    return jnp.einsum("nt,ntf->nf", pool_weights(ids), hidden, precision=HIGH)


def residual_pool(states, ids):
    return jnp.einsum("nt,ntd->nd", pool_weights(ids), states.astype(jnp.float32), precision=HIGH)


def backward_block(states, ids, inner, norm_gain_vector, root_mean_square, hidden_grad):
    count, length, width = states.shape
    input_float = states.astype(jnp.float32).reshape(count * length, width)
    input_normalized, normalized_rows = apply_rms_norm(
        input_float, norm_gain_vector, root_mean_square
    )
    pre = jnp.dot(normalized_rows, inner, preferred_element_type=jnp.float32)
    weights = pool_weights(ids)
    slope = gelu_slope(pre).reshape(count, length, -1)
    dpre = (
        (weights[:, :, None] * hidden_grad[:, None, :] * slope)
        .reshape(count * length, -1)
        .astype(jnp.bfloat16)
    )
    inner_layer_grad = lax.dot_general(
        normalized_rows, dpre, (((0,), (0,)), ((), ())), preferred_element_type=jnp.float32
    )
    normalized_grad = lax.dot_general(
        dpre, inner, (((1,), (1,)), ((), ())), preferred_element_type=jnp.float32
    )
    return (inner_layer_grad, jnp.sum(input_normalized * normalized_grad, axis=0))


def per_device(
    question_states,
    question_ids,
    q_inner_weight,
    q_outer_weight,
    q_norm_gain,
    sql_states,
    sql_ids,
    s_inner_weight,
    s_outer_weight,
    s_norm_gain,
    positive_column,
):
    scale = 1.0 / math.sqrt(D)
    q_table = question_ids[0]
    s_table = sql_ids[0]
    q_rows = q_table.shape[0]
    s_rows = s_table.shape[0]
    own_count = question_states.shape[1]
    q_place = lax.axis_index("sa")
    s_place = lax.axis_index("pb")

    def s_forward(piece):
        pooled = forward_block(piece[0], s_table, s_inner_weight, s_norm_gain, True)
        return pooled

    ids = q_table
    pooled = forward_block(
        lax.all_gather(question_states, "sa", axis=1, tiled=True)[0],
        ids,
        q_inner_weight,
        q_norm_gain,
        False,
    )
    s_pooled = s_forward(lax.all_gather(sql_states, "pb", axis=1, tiled=True))
    q_first = q_place * own_count
    s_first = s_place * own_count
    q_own = residual_pool(
        question_states[0], lax.dynamic_slice_in_dim(q_table, q_first, own_count, 0)
    )
    s_own = residual_pool(sql_states[0], lax.dynamic_slice_in_dim(s_table, s_first, own_count, 0))
    q_resid = lax.dynamic_update_slice_in_dim(
        jnp.zeros((q_rows, D), jnp.float32), q_own, q_first, 0
    )
    s_resid = lax.dynamic_update_slice_in_dim(
        jnp.zeros((s_rows, D), jnp.float32), s_own, s_first, 0
    )
    q_outer_f = q_outer_weight.astype(jnp.float32)
    s_outer_f = s_outer_weight.astype(jnp.float32)
    q_embed = lax.psum(jnp.dot(pooled, q_outer_f, precision=HIGH) + q_resid, "sa")
    s_embed = lax.psum(jnp.dot(s_pooled, s_outer_f, precision=HIGH) + s_resid, "pb")
    tile = scale * lax.dot_general(q_embed, s_embed, (((1,), (1,)), ((), ())), precision=HIGH)
    columns = q_place * s_rows + jnp.arange(s_rows, dtype=jnp.int32)
    match = (positive_column[:, None] == columns[None, :]).astype(jnp.float32)
    row_top = lax.pmax(jnp.max(tile, axis=1), "sa")
    row_total, row_pos = lax.psum(
        (jnp.sum(jnp.exp(tile - row_top[:, None]), axis=1), jnp.sum(match * tile, axis=1)), "sa"
    )
    col_top = lax.pmax(jnp.max(tile, axis=0), "pb")
    col_total, col_pos = lax.psum(
        (jnp.sum(jnp.exp(tile - col_top[None, :]), axis=0), jnp.sum(match * tile, axis=0)), "pb"
    )
    row_lse = row_top + jnp.log(row_total)
    col_lse = col_top + jnp.log(col_total)
    pairs = q_rows * lax.axis_size("pb")
    row_part = jnp.where(q_place == 0, jnp.sum(row_lse - row_pos), 0.0)
    col_part = jnp.where(s_place == 0, jnp.sum(col_lse - col_pos), 0.0)
    loss_part = (row_part + col_part) / (2.0 * pairs)
    dscore = 0.5 * (
        jnp.exp(tile - row_lse[:, None]) + jnp.exp(tile - col_lse[None, :]) - 2.0 * match
    )
    q_grad = lax.psum(scale * jnp.dot(dscore, s_embed, precision=HIGH), "sa")
    s_grad = lax.psum(
        scale * lax.dot_general(dscore, q_embed, (((0,), (0,)), ((), ())), precision=HIGH), "pb"
    )
    q_outer_part = lax.dot_general(pooled, q_grad, (((0,), (0,)), ((), ())), precision=HIGH)
    s_outer_part = lax.dot_general(s_pooled, s_grad, (((0,), (0,)), ((), ())), precision=HIGH)
    q_hidden_grad = lax.dot_general(q_grad, q_outer_f, (((1,), (1,)), ((), ())), precision=HIGH)
    s_hidden_grad = lax.dot_general(s_grad, s_outer_f, (((1,), (1,)), ((), ())), precision=HIGH)

    def s_backward(piece):
        inner_layer_grad, gain_grad = backward_block(
            piece[0], s_table, s_inner_weight, s_norm_gain, True, s_hidden_grad
        )
        return (inner_layer_grad, gain_grad)

    ids = q_table
    inner_layer_grad, gain_grad = backward_block(
        lax.all_gather(question_states, "sa", axis=1, tiled=True)[0],
        ids,
        q_inner_weight,
        q_norm_gain,
        False,
        q_hidden_grad,
    )
    s_inner_part, s_gain_part = s_backward(lax.all_gather(sql_states, "pb", axis=1, tiled=True))
    q_inner_grad, q_outer_grad = lax.psum((inner_layer_grad, q_outer_part), "pb")
    s_inner_grad, s_outer_grad = lax.psum((s_inner_part, s_outer_part), "sa")
    q_gain_grad, s_gain_grad, loss = lax.psum((gain_grad, s_gain_part, loss_part), ("pb", "sa"))
    return (loss, q_inner_grad, q_outer_grad, q_gain_grad, s_inner_grad, s_outer_grad, s_gain_grad)


def solution(mesh):
    placed = (
        P("pb", "sa", None, None),
        P("pb", None, None),
        P(None, "sa"),
        P("sa", None),
        P(),
        P("sa", "pb", None, None),
        P("sa", None, None),
        P(None, "pb"),
        P("pb", None),
        P(),
        P("pb"),
    )
    return jax.shard_map(
        per_device,
        mesh=mesh,
        in_specs=placed,
        out_specs=(P(), P(None, "sa"), P("sa", None), P(), P(None, "pb"), P("pb", None), P()),
        check_vma=False,
    )
```

profile of v0, /device:TPU:1, one launch (start us, length us, event | category | flops | bytes accessed | tf_op | source)
XLA Modules:
  0.0 849.9 jit_solution(1982385561405561287)
XLA Ops:
  15.7 43.4 %all-gather.3.cloned.1.call-done = bf16[1,16,256,768]{3,2,0,1:T(8,128)(2,1)} async-done(((bf16[1,1,256,768]{3,2,0,1:T(8,128)(2,1)}), bf16[1,16,256,768]{3,2,0,1:T(8,128)(2,1)}) %all-gather.3.cloned.1.call-update) | async-done | bytes 6291472 | tf_op jit(solution)/shard_map/all_gather | solution.py:108
  59.1 3.8 convert_reduce_fusion
  70.5 2.7 fusion.16
  74.9 56.9 %psum.105 = f32[16,768]{1,0:T(8,128)S(1)} all-reduce(f32[16,768]{1,0:T(8,128)S(1)} %add.105), channel_id=1, replica_groups=mesh['pb'=16,'sa'=16] {'sa'}, use_global_device_ids=true, to_apply=%region_4.0 | all-reduce | flops 12288 | bytes 98304 | tf_op jit(solution)/shard_map/psum | solution.py:129
  131.7 27.8 %all-gather.5.cloned.1.call-done = bf16[1,16,256,768]{3,2,0,1:T(8,128)(2,1)} async-done(((bf16[1,1,256,768]{3,2,0,1:T(8,128)(2,1)}), bf16[1,16,256,768]{3,2,0,1:T(8,128)(2,1)}) %all-gather.5.cloned.1.call-update) | async-done | bytes 6291472 | tf_op jit(solution)/shard_map/all_gather | solution.py:114
  159.5 4.2 multiply_reduce_fusion.2
  165.9 3.6 multiply_multiply_fusion.2
  169.6 2.7 fusion.13
  174.8 67.6 %psum.106 = f32[16,768]{1,0:T(8,128)} all-reduce(f32[16,768]{1,0:T(8,128)S(1)} %add.109), channel_id=1, replica_groups=mesh['pb'=16,'sa'=16] {'pb'}, use_global_device_ids=true, to_apply=%region_8.0 | all-reduce | flops 12288 | bytes 98304 | tf_op jit(solution)/shard_map/psum | solution.py:130
  243.6 41.3 %pmax.14 = f32[16]{0:T(128)S(1)} all-reduce(f32[16]{0:T(128)S(1)} %get-tuple-element.12), channel_id=1, replica_groups=mesh['pb'=16,'sa'=16] {'sa'}, use_global_device_ids=true, to_apply=%region_10.0 | all-reduce | flops 16 | bytes 128 | tf_op jit(solution)/shard_map/pmax | solution.py:134
  284.9 32.1 %pmax.15 = f32[16]{0:T(128)S(1)} all-reduce(f32[16]{0:T(128)S(1)} %get-tuple-element.11), channel_id=1, replica_groups=mesh['pb'=16,'sa'=16] {'pb'}, use_global_device_ids=true, to_apply=%region_17.0 | all-reduce | flops 16 | bytes 128 | tf_op jit(solution)/shard_map/pmax | solution.py:138
  318.3 34.1 %psum.107 = f32[16]{0:T(128)S(1)} all-reduce(f32[16]{0:T(128)S(1)} %get-tuple-element.10), channel_id=1, replica_groups=mesh['pb'=16,'sa'=16] {'sa'}, use_global_device_ids=true, to_apply=%region_12.0 | all-reduce | flops 16 | bytes 128 | tf_op jit(solution)/shard_map/psum | solution.py:135
  352.4 34.7 %psum.109 = f32[16]{0:T(128)S(1)} all-reduce(f32[16]{0:T(128)S(1)} %get-tuple-element.9), channel_id=1, replica_groups=mesh['pb'=16,'sa'=16] {'pb'}, use_global_device_ids=true, to_apply=%region_19.0 | all-reduce | flops 16 | bytes 128 | tf_op jit(solution)/shard_map/psum | solution.py:139
  390.5 56.9 %all-reduce.1 = (f32[16]{0:T(128)}, f32[16,768]{1,0:T(8,128)S(1)}) all-reduce(f32[16]{0:T(128)} %get-tuple-element.8, f32[16,768]{1,0:T(8,128)} %convolution_multiply_fusion.1), channel_id=1, replica_groups=mesh['pb'=16,'sa'=16] {'sa'}, use_global_device_ids=true, to_apply=%region_14.0 | all-reduce | flops 12304 | bytes 98432 | tf_op jit(solution)/shard_map/psum | solution.py:135
  451.4 4.4 copy.39
  455.8 63.2 %all-reduce.3 = (f32[16]{0:T(128)}, f32[16,768]{1,0:T(8,128)S(1)}) all-reduce(f32[16]{0:T(128)} %get-tuple-element.7, f32[16,768]{1,0:T(8,128)S(1)} %copy-done.27), channel_id=1, replica_groups=mesh['pb'=16,'sa'=16] {'pb'}, use_global_device_ids=true, to_apply=%region_21.0 | all-reduce | flops 12304 | bytes 98432 | tf_op jit(solution)/shard_map/psum | solution.py:139
  520.8 4.5 copy.42
  530.3 2.8 fusion.12
  534.6 5.0 fusion.66
  539.8 5.9 multiply_reduce_fusion
  548.2 4.8 multiply_reduce_fusion.1
  553.1 89.9 %all-reduce = (f32[]{:T(128)}, f32[768]{0:T(1024)}, f32[768]{0:T(1024)}) all-reduce(f32[]{:T(128)S(6)} %div.107, f32[768]{0:T(1024)S(1)} %multiply_reduce_fusion.1, f32[768]{0:T(1024)S(1)} %multiply_reduce_fusion), channel_id=1, replica_groups=mesh['pb'=16,'sa'=16] {'pb','sa'}, use_global_device_ids=true, to_apply=%region_23.24 | all-reduce | flops 1537 | bytes 12296 | tf_op jit(solution)/shard_map/psum | solution.py:178
  643.0 57.8 %all-reduce.10.cloned.1.call-done = (f32[768,192]{0,1:T(8,128)}, f32[192,768]{1,0:T(8,128)}) async-done(((f32[768,192]{0,1:T(8,128)}, f32[192,768]{1,0:T(8,128)}), (f32[768,192]{0,1:T(8,128)}, f32[192,768]{1,0:T(8,128)})) %all-reduce.10.cloned.1.call-update) | async-done | bytes 1179664 | tf_op jit(solution)/shard_map/psum | solution.py:176
  700.8 135.9 %all-reduce.8.cloned.1.call-done = (f32[768,192]{0,1:T(8,128)}, f32[192,768]{1,0:T(8,128)}) async-done(((f32[768,192]{0,1:T(8,128)}, f32[192,768]{1,0:T(8,128)}), (f32[768,192]{0,1:T(8,128)}, f32[192,768]{1,0:T(8,128)})) %all-reduce.8.cloned.1.call-update) | async-done | bytes 1179664 | tf_op jit(solution)/shard_map/psum | solution.py:177
  (135 shorter events, 46.8 us)
Async XLA Ops:
  7.2 158.7 %copy-start = (bf16[768,192]{0,1:T(8,128)(2,1)S(1)}, bf16[768,192]{0,1:T(8,128)(2,1)}, u32[]{:S(2)}) copy-start(bf16[768,192]{0,1:T(8,128)(2,1)} %param.18) | copy-start | bytes 884740
  7.2 51.9 %all-gather.3.cloned.1.call-start = ((), (), s32[]{:S(2)}) async-start(), calls=%async_computation | async-start | bytes 6684672 | tf_op jit(solution)/shard_map/all_gather | solution.py:108
  7.9 151.6 %all-gather.5.cloned.1.call-start = ((), (), s32[]{:S(2)}) async-start(), calls=%async_computation.1 | async-start | bytes 6684672 | tf_op jit(solution)/shard_map/all_gather | solution.py:114
  8.7 692.1 %all-reduce.10.cloned.1.call-start = ((), (), s32[]{:S(2)}) async-start(), calls=%async_computation.3 | async-start | bytes 2359296 | tf_op jit(solution)/shard_map/psum | solution.py:176
  59.1 4.6 copy-start.1
  131.7 32.7 %copy-start.29 = (f32[768]{0:T(1024)S(1)}, f32[768]{0:T(1024)}, u32[]{:S(2)}) copy-start(f32[768]{0:T(1024)} %param.20) | copy-start | bytes 9220
  159.5 4.9 copy-start.4
  165.9 3.7 copy-start.3
  352.4 38.1 %copy-start.34 = (f32[16]{0:T(128)}, f32[16]{0:T(128)S(1)}, u32[]{:S(2)}) copy-start(f32[16]{0:T(128)S(1)} %log_add_fusion.1) | copy-start | bytes 196
  451.4 4.4 copy-start.27
  520.7 4.6 copy-start.6
  520.7 4.6 copy-start.19
  520.8 7.1 slice-start
  530.2 306.5 %all-reduce.8.cloned.1.call-start = ((), (), s32[]{:S(2)}) async-start(), calls=%async_computation.2 | async-start | bytes 2359296 | tf_op jit(solution)/shard_map/psum | solution.py:177
  534.6 5.1 copy-start.26
  539.7 6.0 copy-start.30
  539.7 6.0 copy-start.35
  539.7 7.2 copy-start.31
  539.7 7.2 copy-start.33
  539.7 8.5 copy-start.10
  539.7 8.5 copy-start.16
  539.7 8.5 copy-start.22
  539.7 8.5 copy-start.24
  836.7 5.8 copy-start.14
  (18 other events, 41.1 us)
Sparse Core Ops, SparseCore 0:
  9.9 49.1 all-gather.2
  61.5 97.9 all-gather.4
  530.3 170.4 all-reduce.9
  703.9 132.7 all-reduce.7
where the time goes:
time: 851 us; the launch traced here: 850 us
  blocking collectives  477 us (56%)
  waiting for transfers between devices  266 us (31%)
  matrix products  43.3 us (5%)
  other arithmetic  26 us (3%)
  local copies, waits for them, and re-layouts  20.5 us (2%)
  between operations  17 us (2%)
    psum x1, waiting for transfers between devices, per_device(): s_inner_grad, s_outer_grad = lax.psum((s_inner_part, s_outer_part), 'sa')  136 us
    psum x2, blocking collectives, per_device(): lax.psum((jnp.sum(jnp.exp(tile - col_top[None, :]), axis=0), jnp.sum(matc...  97.9 us
    psum x2, blocking collectives, per_device(): lax.psum((jnp.sum(jnp.exp(tile - row_top[:, None]), axis=1), jnp.sum(matc...  91 us
    psum x1, blocking collectives, per_device(): lax.psum((gain_grad, s_gain_part, loss_part), ('pb', 'sa'))  89.9 us
    psum x1, blocking collectives, per_device(): lax.psum(jnp.dot(s_pooled, s_outer_f, precision=HIGH) + s_resid, 'pb')  67.6 us
    psum x1, waiting for transfers between devices, per_device(): lax.psum((inner_layer_grad, q_outer_part), 'pb')  57.8 us
    psum x1, blocking collectives, per_device(): lax.psum(jnp.dot(pooled, q_outer_f, precision=HIGH) + q_resid, 'sa')  56.9 us
    all_gather x1, waiting for transfers between devices, per_device(): lax.all_gather(question_states, 'sa', axis=1, tiled=True)[0]  43.4 us
  transfers between devices with their start and end apart: 4, of which 4 were waited for; matrix products, arithmetic and copies ran while one was open for 5% of the time, Pallas kernels for 0%

commit v1 on v0

v1 whole, which is shorter than its diff:
```python
import math

import jax
import jax.numpy as jnp
from jax import lax
from jax.sharding import PartitionSpec as P

D = 768


HIGH = lax.Precision.HIGHEST


def apply_rms_norm(input_float, norm_gain_vector, root_mean_square):
    if root_mean_square:
        input_normalized = input_float * lax.rsqrt(
            jnp.mean(input_float * input_float, axis=-1, keepdims=True) + 1e-06
        )
    else:
        mean_removed = input_float - jnp.mean(input_float, axis=-1, keepdims=True)
        input_normalized = mean_removed * lax.rsqrt(
            jnp.mean(mean_removed * mean_removed, axis=-1, keepdims=True) + 1e-05
        )
    return (input_normalized, (input_normalized * norm_gain_vector).astype(jnp.bfloat16))


def gelu_value(v):
    return 0.5 * v * (1.0 + lax.erf(v / math.sqrt(2.0)))


def gelu_slope(v):
    return 0.5 * (1.0 + lax.erf(v / math.sqrt(2.0))) + v * jnp.exp(-0.5 * v * v) / math.sqrt(
        2.0 * math.pi
    )


def pool_weights(ids):
    mask = (ids > 0).astype(jnp.float32)
    return mask / jnp.sum(mask, axis=-1, keepdims=True)


def tower_forward(tokens, ids, inner, gain, root_mean_square):
    count, length, width = tokens.shape
    input_float = tokens.astype(jnp.float32).reshape(count * length, width)
    input_normalized, normalized_rows = apply_rms_norm(input_float, gain, root_mean_square)
    pre = jnp.dot(normalized_rows, inner, preferred_element_type=jnp.float32)
    weights = pool_weights(ids)
    hidden = gelu_value(pre).reshape(count, length, -1)
    pooled = jnp.einsum("nt,ntf->nf", weights, hidden, precision=HIGH)
    resid = jnp.einsum(
        "nt,ntd->nd", weights, input_float.reshape(count, length, width), precision=HIGH
    )
    return input_normalized, normalized_rows, pre, weights, pooled, resid


def tower_backward(input_normalized, normalized_rows, pre, weights, inner, hidden_grad):
    count, length = weights.shape
    slope = gelu_slope(pre).reshape(count, length, -1)
    dpre = (
        (weights[:, :, None] * hidden_grad[:, None, :] * slope)
        .reshape(count * length, -1)
        .astype(jnp.bfloat16)
    )
    inner_part = lax.dot_general(
        normalized_rows, dpre, (((0,), (0,)), ((), ())), preferred_element_type=jnp.float32
    )
    normalized_grad = lax.dot_general(
        dpre, inner, (((1,), (1,)), ((), ())), preferred_element_type=jnp.float32
    )
    return inner_part, jnp.sum(input_normalized * normalized_grad, axis=0)


def per_device(
    question_states,
    question_ids,
    q_inner_weight,
    q_outer_weight,
    q_norm_gain,
    sql_states,
    sql_ids,
    s_inner_weight,
    s_outer_weight,
    s_norm_gain,
    positive_column,
):
    scale = 1.0 / math.sqrt(D)
    q_place = lax.axis_index("sa")
    s_place = lax.axis_index("pb")
    q_tokens = lax.all_gather(question_states, "sa", axis=1, tiled=True)[0]
    s_tokens = lax.all_gather(sql_states, "pb", axis=1, tiled=True)[0]
    q_rows = q_tokens.shape[0]
    s_rows = s_tokens.shape[0]

    q_hat, q_normed, q_pre, q_weights, q_pooled, q_resid = tower_forward(
        q_tokens, question_ids[0], q_inner_weight, q_norm_gain, False
    )
    s_hat, s_normed, s_pre, s_weights, s_pooled, s_resid = tower_forward(
        s_tokens, sql_ids[0], s_inner_weight, s_norm_gain, True
    )
    q_outer_f = q_outer_weight.astype(jnp.float32)
    s_outer_f = s_outer_weight.astype(jnp.float32)
    q_block = lax.psum(jnp.dot(q_pooled, q_outer_f, precision=HIGH), "sa") + q_resid
    s_block = lax.psum(jnp.dot(s_pooled, s_outer_f, precision=HIGH), "pb") + s_resid
    q_embed = lax.all_gather(q_block, "pb", axis=0, tiled=True)
    s_embed = lax.all_gather(s_block, "sa", axis=0, tiled=True)
    q_pooled_all = lax.all_gather(q_pooled, "pb", axis=0, tiled=True)
    s_pooled_all = lax.all_gather(s_pooled, "sa", axis=0, tiled=True)
    positive_all = lax.all_gather(positive_column, "pb", axis=0, tiled=True)

    score = scale * lax.dot_general(q_embed, s_embed, (((1,), (1,)), ((), ())), precision=HIGH)
    count = score.shape[0]
    match = (positive_all[:, None] == jnp.arange(count, dtype=jnp.int32)[None, :]).astype(
        jnp.float32
    )
    row_max = jnp.max(score, axis=1)
    row_lse = row_max + jnp.log(jnp.sum(jnp.exp(score - row_max[:, None]), axis=1))
    col_max = jnp.max(score, axis=0)
    col_lse = col_max + jnp.log(jnp.sum(jnp.exp(score - col_max[None, :]), axis=0))
    row_pos = jnp.sum(match * score, axis=1)
    col_pos = jnp.sum(match * score, axis=0)
    loss = (jnp.sum(row_lse - row_pos) + jnp.sum(col_lse - col_pos)) / (2.0 * count)
    dscore = 0.5 * (
        jnp.exp(score - row_lse[:, None]) + jnp.exp(score - col_lse[None, :]) - 2.0 * match
    )
    q_grad = scale * jnp.dot(dscore, s_embed, precision=HIGH)
    s_grad = scale * lax.dot_general(dscore, q_embed, (((0,), (0,)), ((), ())), precision=HIGH)

    q_outer_grad = lax.dot_general(q_pooled_all, q_grad, (((0,), (0,)), ((), ())), precision=HIGH)
    s_outer_grad = lax.dot_general(s_pooled_all, s_grad, (((0,), (0,)), ((), ())), precision=HIGH)
    q_grad_own = lax.dynamic_slice_in_dim(q_grad, s_place * q_rows, q_rows, 0)
    s_grad_own = lax.dynamic_slice_in_dim(s_grad, q_place * s_rows, s_rows, 0)
    q_hidden_grad = lax.dot_general(
        q_grad_own, q_outer_f, (((1,), (1,)), ((), ())), precision=HIGH
    )
    s_hidden_grad = lax.dot_general(
        s_grad_own, s_outer_f, (((1,), (1,)), ((), ())), precision=HIGH
    )
    q_inner_part, q_gain_part = tower_backward(
        q_hat, q_normed, q_pre, q_weights, q_inner_weight, q_hidden_grad
    )
    s_inner_part, s_gain_part = tower_backward(
        s_hat, s_normed, s_pre, s_weights, s_inner_weight, s_hidden_grad
    )
    q_inner_grad = lax.psum(q_inner_part, "pb")
    s_inner_grad = lax.psum(s_inner_part, "sa")
    q_gain_grad, s_gain_grad = lax.psum((q_gain_part, s_gain_part), ("pb", "sa"))
    return (loss, q_inner_grad, q_outer_grad, q_gain_grad, s_inner_grad, s_outer_grad, s_gain_grad)


def solution(mesh):
    placed = (
        P("pb", "sa", None, None),
        P("pb", None, None),
        P(None, "sa"),
        P("sa", None),
        P(),
        P("sa", "pb", None, None),
        P("sa", None, None),
        P(None, "pb"),
        P("pb", None),
        P(),
        P("pb"),
    )
    return jax.shard_map(
        per_device,
        mesh=mesh,
        in_specs=placed,
        out_specs=(P(), P(None, "sa"), P("sa", None), P(), P(None, "pb"), P("pb", None), P()),
        check_vma=False,
    )
```

time: 851 us -> 713 us (0.84); the launches traced: 850 us -> 703 us
  blocking collectives: 477 us -> 351 us
  waiting for transfers between devices: 266 us -> 245 us
    psum x7 -> x3, blocking collectives: 403 us -> 200 us  [the longest x1 82.2 us: per_device(): lax.psum((q_gain_part, s_gain_part), ('pb', 'sa'))]
    all_gather x0 -> x4, blocking collectives: none -> 131 us  [the longest x1 39.3 us: per_device(): q_embed = lax.all_gather(q_block, 'pb', axis=0, tiled=True)]
    pmax x2 -> x0, blocking collectives: 73.4 us -> none  [the longest x1 41.3 us: per_device(): row_top = lax.pmax(jnp.max(tile, axis=1), 'sa')]
    psum x2, waiting for transfers between devices: 194 us -> 125 us  [the longest x1 125 us: per_device(): s_inner_grad = lax.psum(s_inner_part, 'sa')]
    all_gather x2, waiting for transfers between devices: 71.2 us -> 119 us  [the longest x1 70.7 us: per_device(): s_tokens = lax.all_gather(sql_states, 'pb', axis=1, tiled=True)[0]]
    unnamed x0 -> x1, blocking collectives: none -> 19.8 us
    unnamed x89 -> x86, local copies, waits for them, and re-layouts: 18.8 us -> 16.4 us
  transfers between devices with their start and end apart: 4 -> 4, of which waited for: 4 -> 3; matrix products, arithmetic and copies ran while one was open for 5% -> 5% of each run, Pallas kernels for 0% -> 0%
where the time goes in v1:
time: 713 us; the launch traced here: 703 us
  blocking collectives  351 us (49%)
  waiting for transfers between devices  245 us (34%)
  matrix products  45.8 us (6%)
  other arithmetic  25 us (4%)
  local copies, waits for them, and re-layouts  18.6 us (3%)
  between operations  17.6 us (2%)
    psum x1, waiting for transfers between devices, per_device(): s_inner_grad = lax.psum(s_inner_part, 'sa')  125 us
    psum x1, blocking collectives, per_device(): lax.psum((q_gain_part, s_gain_part), ('pb', 'sa'))  82.2 us
    all_gather x1, waiting for transfers between devices, per_device(): s_tokens = lax.all_gather(sql_states, 'pb', axis=1, tiled=True)[0]  70.7 us
    psum x1, blocking collectives, per_device(): lax.psum(jnp.dot(s_pooled, s_outer_f, precision=HIGH), 'pb') + s_resid  69.4 us
    psum x1, blocking collectives, per_device(): lax.psum(jnp.dot(q_pooled, q_outer_f, precision=HIGH), 'sa') + q_resid  48.9 us
    all_gather x1, waiting for transfers between devices, per_device(): q_tokens = lax.all_gather(question_states, 'sa', axis=1, tiled=True)[0]  47.9 us
    all_gather x1, blocking collectives, per_device(): q_embed = lax.all_gather(q_block, 'pb', axis=0, tiled=True)  39.3 us
    all_gather x1, blocking collectives, per_device(): s_embed = lax.all_gather(s_block, 'sa', axis=0, tiled=True)  36.3 us
  transfers between devices with their start and end apart: 4, of which 3 were waited for; matrix products, arithmetic and copies ran while one was open for 5% of the time, Pallas kernels for 0%

profile of v1, /device:TPU:1, one launch (start us, length us, event | category | flops | bytes accessed | tf_op | source)
XLA Modules:
  0.0 703.2 jit_solution(16623077752459873952)
XLA Ops:
  14.6 19.8 %all-reduce = s32[256]{0:T(256)} all-reduce(s32[256]{0:T(256)S(1)} %dynamic-update-slice), channel_id=1, replica_groups=mesh['pb'=16,'sa'=16] {'pb'}, use_global_device_ids=true, to_apply=%add | all-reduce | flops 256 | bytes 2048
  34.4 70.7 %all-gather.5.cloned.1.call-done = bf16[1,16,256,768]{3,2,0,1:T(8,128)(2,1)} async-done(((bf16[1,1,256,768]{3,2,0,1:T(8,128)(2,1)}), bf16[1,16,256,768]{3,2,0,1:T(8,128)(2,1)}) %all-gather.5.cloned.1.call-update) | async-done | bytes 6291472 | tf_op jit(solution)/shard_map/all_gather | solution.py:90
  105.1 4.1 multiply_reduce_fusion.2
  109.2 47.9 %all-gather.3.cloned.1.call-done = bf16[1,16,256,768]{3,2,0,1:T(8,128)(2,1)} async-done(((bf16[1,1,256,768]{3,2,0,1:T(8,128)(2,1)}), bf16[1,16,256,768]{3,2,0,1:T(8,128)(2,1)}) %all-gather.3.cloned.1.call-update) | async-done | bytes 6291472 | tf_op jit(solution)/shard_map/all_gather | solution.py:89
  157.2 3.8 convert_reduce_fusion
  166.1 3.8 multiply_multiply_fusion.2
  169.9 2.7 fusion.17
  173.4 69.4 %psum.43 = f32[16,768]{1,0:T(8,128)S(1)} all-reduce(f32[16,768]{1,0:T(8,128)S(1)} %fusion.42), channel_id=1, replica_groups=mesh['pb'=16,'sa'=16] {'pb'}, use_global_device_ids=true, to_apply=%region_6.0 | all-reduce | flops 12288 | bytes 98304 | tf_op jit(solution)/shard_map/psum | solution.py:103
  242.8 5.3 fusion.1
  248.1 36.3 %all_gather.24 = f32[256,768]{1,0:T(8,128)} all-gather(f32[16,768]{1,0:T(8,128)S(1)} %bitcast_add_fusion), channel_id=1, replica_groups=mesh['pb'=16,'sa'=16] {'sa'}, dimensions={0}, use_global_device_ids=true | all-gather | bytes 835584 | tf_op jit(solution)/shard_map/all_gather | solution.py:105
  284.4 4.6 multiply_convert_fusion.1
  295.1 48.9 %psum.42 = f32[16,768]{1,0:T(8,128)S(1)} all-reduce(f32[16,768]{1,0:T(8,128)S(1)} %fusion.41), channel_id=1, replica_groups=mesh['pb'=16,'sa'=16] {'sa'}, use_global_device_ids=true, to_apply=%region_3.0 | all-reduce | flops 12288 | bytes 98304 | tf_op jit(solution)/shard_map/psum | solution.py:102
  344.1 5.4 fusion.3
  349.5 39.3 %all_gather.22 = f32[256,768]{1,0:T(8,128)S(1)} all-gather(f32[16,768]{1,0:T(8,128)S(1)} %bitcast_add_fusion.1), channel_id=1, replica_groups=mesh['pb'=16,'sa'=16] {'pb'}, dimensions={0}, use_global_device_ids=true | all-gather | bytes 835584 | tf_op jit(solution)/shard_map/all_gather | solution.py:104
  394.3 2.7 copy.41
  403.1 4.4 copy.44
  408.9 3.7 fusion.16
  412.9 4.9 multiply_reduce_fusion.1
  417.9 2.8 multiply_reduce_fusion
  420.7 82.2 %all-reduce.1 = (f32[768]{0:T(1024)}, f32[768]{0:T(1024)}) all-reduce(f32[768]{0:T(1024)S(1)} %multiply_reduce_fusion.1, f32[768]{0:T(1024)S(1)} %multiply_reduce_fusion), channel_id=1, replica_groups=mesh['pb'=16,'sa'=16] {'pb','sa'}, use_global_device_ids=true, to_apply=%region_17.0 | all-reduce | flops 1536 | bytes 12288 | tf_op jit(solution)/shard_map/psum | solution.py:146
  502.9 21.3 %all_gather.27 = f32[256,192]{1,0:T(8,128)S(1)} all-gather(f32[16,192]{1,0:T(8,128)S(1)} %bitcast.132), channel_id=1, replica_groups=mesh['pb'=16,'sa'=16] {'sa'}, dimensions={0}, use_global_device_ids=true | all-gather | bytes 208896 | tf_op jit(solution)/shard_map/all_gather | solution.py:107
  524.2 5.5 fusion.47
  529.7 33.7 %all_gather.26 = f32[256,192]{1,0:T(8,128)S(1)} all-gather(f32[16,192]{1,0:T(8,128)S(1)} %bitcast.133), channel_id=1, replica_groups=mesh['pb'=16,'sa'=16] {'pb'}, dimensions={0}, use_global_device_ids=true | all-gather | bytes 208896 | tf_op jit(solution)/shard_map/all_gather | solution.py:106
  566.5 125.0 %all-reduce.7.cloned.1.call-done = f32[768,192]{0,1:T(8,128)} async-done(((f32[768,192]{0,1:T(8,128)}), f32[768,192]{0,1:T(8,128)}) %all-reduce.7.cloned.1.call-update) | async-done | bytes 589840 | tf_op jit(solution)/shard_map/psum | solution.py:145
  (130 shorter events, 37.4 us)
Async XLA Ops:
  7.2 281.8 %copy-start = (bf16[768,192]{0,1:T(8,128)(2,1)S(1)}, bf16[768,192]{0,1:T(8,128)(2,1)}, u32[]{:S(2)}) copy-start(bf16[768,192]{0,1:T(8,128)(2,1)} %param.13) | copy-start | bytes 884740
  7.2 97.9 %all-gather.5.cloned.1.call-start = ((), (), s32[]{:S(2)}) async-start(), calls=%async_computation.1 | async-start | bytes 6684672 | tf_op jit(solution)/shard_map/all_gather | solution.py:90
  7.9 149.3 %all-gather.3.cloned.1.call-start = ((), (), s32[]{:S(2)}) async-start(), calls=%async_computation | async-start | bytes 6684672 | tf_op jit(solution)/shard_map/all_gather | solution.py:89
  8.7 557.8 %all-reduce.5.cloned.1.call-start = ((), (), s32[]{:S(2)}) async-start(), calls=%async_computation.2 | async-start | bytes 1179648 | tf_op jit(solution)/shard_map/psum | solution.py:144
  109.2 54.6 %copy-start.19 = (f32[2,2,8,128]{3,1,2,0:T(2,128)}, f32[2,2,8,128]{3,1,2,0:T(2,128)S(1)}, u32[]{:S(2)}) copy-start(f32[2,2,8,128]{3,1,2,0:T(2,128)S(1)} %copy.38) | copy-start | bytes 49156
  161.1 123.3 %copy-start.21 = (f32[2,2,8,128]{3,1,2,0:T(2,128)}, f32[2,2,8,128]{3,1,2,0:T(2,128)S(1)}, u32[]{:S(2)}) copy-start(f32[2,2,8,128]{3,1,2,0:T(2,128)S(1)} %copy.36) | copy-start | bytes 49156
  163.8 120.6 %copy-start.23 = (f32[2,2,8,128]{3,1,2,0:T(2,128)}, f32[2,2,8,128]{3,1,2,0:T(2,128)S(1)}, u32[]{:S(2)}) copy-start(f32[2,2,8,128]{3,1,2,0:T(2,128)S(1)} %copy.37) | copy-start | bytes 49156
  242.8 41.6 %copy-start.29 = (f32[768]{0:T(1024)S(1)}, f32[768]{0:T(1024)}, u32[]{:S(2)}) copy-start(f32[768]{0:T(1024)} %param.15) | copy-start | bytes 9220
  344.1 44.7 %copy-start.5 = (f32[256,768]{1,0:T(8,128)S(1)}, f32[256,768]{1,0:T(8,128)}, u32[]{:S(2)}) copy-start(f32[256,768]{1,0:T(8,128)} %all_gather.24) | copy-start | bytes 2359300
  344.1 45.6 %copy-start.27 = (s32[256]{0:T(256)S(1)}, s32[256]{0:T(256)}, u32[]{:S(2)}) copy-start(s32[256]{0:T(256)} %all-reduce) | copy-start | bytes 3076
  349.5 43.9 %copy-start.12 = (bf16[192,768]{1,0:T(8,128)(2,1)S(1)}, bf16[192,768]{1,0:T(8,128)(2,1)}, u32[]{:S(2)}) copy-start(bf16[192,768]{1,0:T(8,128)(2,1)} %param.14) | copy-start | bytes 884740
  394.3 5.4 slice-start.4
  402.0 289.6 %all-reduce.7.cloned.1.call-start = ((), (), s32[]{:S(2)}) async-start(), calls=%async_computation.3 | async-start | bytes 1179648 | tf_op jit(solution)/shard_map/psum | solution.py:145
  403.1 5.8 copy-start.17
  403.1 9.5 %slice-start = ((s8[6291456]{0:T(1024)(128)(4,1)}), s8[2097152]{0:T(1024)(128)(4,1)S(1)}, s32[]{:S(2)}) async-start(s8[6291456]{0:T(1024)(128)(4,1)} %bitcast.112), calls=%async_computation.4 | async-start | bytes 4194304
  403.1 9.5 %copy-start.22 = (f32[2,2,8,128]{3,1,2,0:T(2,128)S(1)}, f32[2,2,8,128]{3,1,2,0:T(2,128)}, u32[]{:S(2)}) copy-start(f32[2,2,8,128]{3,1,2,0:T(2,128)} %copy-done.21) | copy-start | bytes 49156
  403.1 9.5 %copy-start.24 = (f32[2,2,8,128]{3,1,2,0:T(2,128)S(1)}, f32[2,2,8,128]{3,1,2,0:T(2,128)}, u32[]{:S(2)}) copy-start(f32[2,2,8,128]{3,1,2,0:T(2,128)} %copy-done.23) | copy-start | bytes 49156
  408.9 9.0 %slice-start.2 = ((s8[6291456]{0:T(1024)(128)(4,1)}), s8[4194304]{0:T(1024)(128)(4,1)S(1)}, s32[]{:S(2)}) async-start(s8[6291456]{0:T(1024)(128)(4,1)} %bitcast.114), calls=%async_computation.6 | async-start | bytes 8388608
  412.9 5.0 slice-start.3
  412.9 5.0 copy-start.16
  412.9 5.0 copy-start.20
  417.9 85.0 %copy-start.25 = (f32[16,1,192]{2,0,1:T(8,128)S(1)}, f32[16,1,192]{2,0,1:T(8,128)}, u32[]{:S(2)}) copy-start(f32[16,1,192]{2,0,1:T(8,128)} %copy.67) | copy-start | bytes 36868
  524.2 5.6 copy-start.26
  524.2 40.8 %copy-start.7 = (f32[256,768]{1,0:T(8,128)S(1)}, f32[256,768]{1,0:T(8,128)}, u32[]{:S(2)}) copy-start(f32[256,768]{1,0:T(8,128)} %copy-done.6) | copy-start | bytes 2359300
  (16 other events, 47.3 us)
Sparse Core Ops, SparseCore 0:
  10.5 94.5 all-gather.4
  107.0 50.1 all-gather.2
  402.1 159.9 all-reduce.4
  565.3 126.1 all-reduce.6

commit v2 on v1

--- a/solution.py
+++ b/solution.py
@@ -1,11 +1,80 @@
+import functools
 import math
 
 import jax
 import jax.numpy as jnp
 from jax import lax
+from jax.experimental import pallas as pl
+from jax.experimental.pallas import tpu as pltpu
 from jax.sharding import PartitionSpec as P
 
 D = 768
+
+MESH_AXES = ("pb", "sa")
+
+
+def _peer(axis, p):
+    return tuple(p if a == axis else lax.axis_index(a) for a in MESH_AXES)
+
+
+def exchange(jobs, cid):
+    arrays = [a for a, _, _ in jobs]
+    kinds = [(ax, spread) for _, ax, spread in jobs]
+    sizes = {ax: lax.axis_size(ax) for ax, _ in kinds}
+    widest = max(sizes.values())
+    count = len(jobs)
+
+    def kernel(*refs):
+        srcs, dsts = refs[:count], refs[count:2 * count]
+        send, recv, local = refs[2 * count:]
+        barrier = pltpu.get_barrier_semaphore()
+        axes = list(dict.fromkeys(ax for ax, _ in kinds))
+        total = 0
+        for ax in axes:
+            n = sizes[ax]
+            me = lax.axis_index(ax)
+            for s in range(1, n):
+                pl.semaphore_signal(barrier, 1, device_id=_peer(ax, lax.rem(me + s, n)),
+                                    device_id_type=pl.DeviceIdType.MESH)
+            total += n - 1
+        pl.semaphore_wait(barrier, total)
+        started = []
+        for t, (ax, spread) in enumerate(kinds):
+            n = sizes[ax]
+            me = lax.axis_index(ax)
+            for s in range(1, n):
+                p = lax.rem(me + s, n)
+                src = srcs[t].at[p] if spread else srcs[t]
+                c = pltpu.make_async_remote_copy(
+                    src_ref=src, dst_ref=dsts[t].at[me], send_sem=send.at[t, s],
+                    recv_sem=recv.at[t, s], device_id=_peer(ax, p),
+                    device_id_type=pl.DeviceIdType.MESH)
+                c.start()
+                started.append(c)
+            src = srcs[t].at[me] if spread else srcs[t]
+            c = pltpu.make_async_copy(src, dsts[t].at[me], local.at[t])
+            c.start()
+            started.append(c)
+        for c in started:
+            c.wait()
+
+    out_shape = []
+    for a, (ax, spread) in zip(arrays, kinds):
+        shape = a.shape if spread else (sizes[ax],) + a.shape
+        out_shape.append(jax.ShapeDtypeStruct(shape, a.dtype))
+    anywhere = pl.BlockSpec(memory_space=pl.ANY)
+    return pl.pallas_call(
+        kernel,
+        out_shape=out_shape,
+        in_specs=[anywhere] * count,
+        out_specs=[anywhere] * count,
+        scratch_shapes=[
+            pltpu.SemaphoreType.DMA((count, widest)),
+            pltpu.SemaphoreType.DMA((count, widest)),
+            pltpu.SemaphoreType.DMA((count,)),
+        ],
+        compiler_params=pltpu.CompilerParams(collective_id=cid, has_side_effects=True),
+    )(*arrays)
 
 
 HIGH = lax.Precision.HIGHEST
@@ -86,8 +155,15 @@
     scale = 1.0 / math.sqrt(D)
     q_place = lax.axis_index("sa")
     s_place = lax.axis_index("pb")
-    q_tokens = lax.all_gather(question_states, "sa", axis=1, tiled=True)[0]
-    s_tokens = lax.all_gather(sql_states, "pb", axis=1, tiled=True)[0]
+    q_tokens, s_tokens, positive_all = exchange(
+        [
+            (question_states[0, 0], "sa", False),
+            (sql_states[0, 0], "pb", False),
+            (positive_column.reshape(1, -1), "pb", False),
+        ],
+        0,
+    )
+    positive_all = positive_all.reshape(-1)
     q_rows = q_tokens.shape[0]
     s_rows = s_tokens.shape[0]
 
@@ -99,14 +175,28 @@
     )
     q_outer_f = q_outer_weight.astype(jnp.float32)
     s_outer_f = s_outer_weight.astype(jnp.float32)
-    q_block = lax.psum(jnp.dot(q_pooled, q_outer_f, precision=HIGH), "sa") + q_resid
-    s_block = lax.psum(jnp.dot(s_pooled, s_outer_f, precision=HIGH), "pb") + s_resid
-    q_embed = lax.all_gather(q_block, "pb", axis=0, tiled=True)
-    s_embed = lax.all_gather(s_block, "sa", axis=0, tiled=True)
-    q_pooled_all = lax.all_gather(q_pooled, "pb", axis=0, tiled=True)
-    s_pooled_all = lax.all_gather(s_pooled, "sa", axis=0, tiled=True)
-    positive_all = lax.all_gather(positive_column, "pb", axis=0, tiled=True)
-
+    q_terms, s_terms = exchange(
+        [
+            (jnp.dot(q_pooled, q_outer_f, precision=HIGH), "sa", False),
+            (jnp.dot(s_pooled, s_outer_f, precision=HIGH), "pb", False),
+        ],
+        1,
+    )
+    q_block = jnp.sum(q_terms, axis=0) + q_resid
+    s_block = jnp.sum(s_terms, axis=0) + s_resid
+    q_embed, q_pooled_all, s_embed, s_pooled_all = exchange(
+        [
+            (q_block, "pb", False),
+            (q_pooled, "pb", False),
+            (s_block, "sa", False),
+            (s_pooled, "sa", False),
+        ],
+        2,
+    )
+    q_embed = q_embed.reshape(-1, D)
+    s_embed = s_embed.reshape(-1, D)
+    q_pooled_all = q_pooled_all.reshape(-1, q_pooled.shape[-1])
+    s_pooled_all = s_pooled_all.reshape(-1, s_pooled.shape[-1])
     score = scale * lax.dot_general(q_embed, s_embed, (((1,), (1,)), ((), ())), precision=HIGH)
     count = score.shape[0]
     match = (positive_all[:, None] == jnp.arange(count, dtype=jnp.int32)[None, :]).astype(
@@ -141,9 +231,24 @@
     s_inner_part, s_gain_part = tower_backward(
         s_hat, s_normed, s_pre, s_weights, s_inner_weight, s_hidden_grad
     )
-    q_inner_grad = lax.psum(q_inner_part, "pb")
-    s_inner_grad = lax.psum(s_inner_part, "sa")
-    q_gain_grad, s_gain_grad = lax.psum((q_gain_part, s_gain_part), ("pb", "sa"))
+    q_pieces = q_inner_part.reshape(lax.axis_size("pb"), -1, q_inner_part.shape[-1])
+    s_pieces = s_inner_part.reshape(lax.axis_size("sa"), -1, s_inner_part.shape[-1])
+    gains = jnp.stack([q_gain_part, s_gain_part])
+    q_pieces, s_pieces, gains = exchange(
+        [(q_pieces, "pb", True), (s_pieces, "sa", True), (gains, "sa", False)], 3
+    )
+    q_inner_grad, s_inner_grad, gains = exchange(
+        [
+            (jnp.sum(q_pieces, axis=0), "pb", False),
+            (jnp.sum(s_pieces, axis=0), "sa", False),
+            (jnp.sum(gains, axis=0), "pb", False),
+        ],
+        4,
+    )
+    q_inner_grad = q_inner_grad.reshape(q_inner_part.shape)
+    s_inner_grad = s_inner_grad.reshape(s_inner_part.shape)
+    gains = jnp.sum(gains, axis=0)
+    q_gain_grad, s_gain_grad = gains[0], gains[1]
     return (loss, q_inner_grad, q_outer_grad, q_gain_grad, s_inner_grad, s_outer_grad, s_gain_grad)
 
 

time: 713 us -> 524 us (0.73)
  Pallas kernels: 0 us -> 393 us
  blocking collectives: 351 us -> 0 us
  waiting for transfers between devices: 245 us -> 0 us
  local copies, waits for them, and re-layouts: 18.6 us -> 33.6 us
  between operations: 17.6 us -> 3.99 us
  matrix products: 45.8 us -> 54.2 us
    pallas_call x0 -> x5, Pallas kernels: none -> 393 us  [exchange(): pl.pallas_call(kernel, out_shape=out_shape, in_specs=[anywhere] * count,...]
    psum x3 -> x0, blocking collectives: 200 us -> none  [the longest x1 82.2 us: per_device(): lax.psum((q_gain_part, s_gain_part), ('pb', 'sa'))]
    all_gather x4 -> x0, blocking collectives: 131 us -> none  [the longest x1 39.3 us: per_device(): q_embed = lax.all_gather(q_block, 'pb', axis=0, tiled=True)]
    psum x2 -> x0, waiting for transfers between devices: 125 us -> none  [the longest x1 125 us: per_device(): s_inner_grad = lax.psum(s_inner_part, 'sa')]
    all_gather x2 -> x0, waiting for transfers between devices: 119 us -> none  [the longest x1 70.7 us: per_device(): s_tokens = lax.all_gather(sql_states, 'pb', axis=1, tiled=True)[0]]
    unnamed x1 -> x0, blocking collectives: 19.8 us -> none
    dot_general x0 -> x2, local copies, waits for them, and re-layouts: none -> 17.5 us  [tower_backward(): lax.dot_general(normalized_rows, dpre, (((0,), (0,)), ((), ())), preferre...]
    reduce_sum x0 -> x7, other arithmetic: none -> 9.06 us  [the longest x1 1.81 us: per_device(): jnp.sum(q_pieces, axis=0)]
  transfers between devices with their start and end apart: 4 -> 0, of which waited for: 3 -> 0; matrix products, arithmetic and copies ran while one was open for 5% -> 0% of each run, Pallas kernels for 0% -> 0%
where the time goes in v2:
time: 524 us; the launch traced here: 515 us
  Pallas kernels  393 us (75%)
  matrix products  54.2 us (10%)
  local copies, waits for them, and re-layouts  33.6 us (6%)
  other arithmetic  30.7 us (6%)
    pallas_call x5, Pallas kernels, exchange(): pl.pallas_call(kernel, out_shape=out_shape, in_specs=[anywhere] * count,...  393 us
    dot_general x2, local copies, waits for them, and re-layouts, tower_backward(): lax.dot_general(normalized_rows, dpre, (((0,), (0,)), ((), ())), preferre...  17.5 us
    unnamed x89, local copies, waits for them, and re-layouts  12.8 us
    dot_general x2, matrix products, tower_backward(): lax.dot_general(normalized_rows, dpre, (((0,), (0,)), ((), ())), preferre...  11 us
    dot_general x2, matrix products, tower_forward(): jnp.einsum('nt,ntd->nd', weights, input_float.reshape(count, length, widt...  10.7 us

profile of v2, /device:TPU:1, one launch (start us, length us, event | category | flops | bytes accessed | tf_op | source)
XLA Modules:
  0.0 515.4 jit_solution(2489246983689496163)
XLA Ops:
  0.6 242.3 %shard_map.162 = (bf16[16,256,768]{2,1,0:T(8,128)(2,1)}, bf16[16,256,768]{2,1,0:T(8,128)(2,1)}, s32[16,1,16]{2,1,0:T(1,128)}) custom-call(bf16[256,768]{1,0:T(8,128)(2,1)} %bitcast.142, bf16[256,768]{1,0:T(8,128)(2,1)} %bitcast.143, s32[1,16]{1,0:T(1,128)} %bitcast.158), custom_call_target="tpu_custom_call" | custom-call | tf_op jit(solution)/shard_map/pallas_call | solution.py:66
  243.0 3.8 convert_reduce_fusion
  251.8 3.6 multiply_convert_fusion
  255.4 2.5 multiply_multiply_fusion.2
  260.0 2.7 fusion.13
  263.5 4.0 multiply_multiply_fusion.3
  269.0 2.7 fusion.16
  272.5 36.1 %shard_map.163 = (f32[16,16,768]{2,1,0:T(8,128)}, f32[16,16,768]{2,1,0:T(8,128)}) custom-call(f32[16,768]{1,0:T(8,128)} %fusion.43.refs_0_, f32[16,768]{1,0:T(8,128)} %fusion.44.refs_1_), custom_call_target="tpu_custom_call" | custom-call | tf_op jit(solution)/shard_map/pallas_call | solution.py:66
  309.8 5.3 %fusion.37 = f32[16,1,768]{2,1,0:T(1,128)S(1)} fusion(bf16[16,256,768]{2,1,0:T(8,128)(2,1)} %get-tuple-element.22, f32[16,256,1]{1,0,2:T(8,128)S(1)} %get-tuple-element.72), kind=kOutput, calls=%fused_computation.71 | convolution fusion | flops 37748736 | bytes 6356992 | tf_op jit(solution)/shard_map/nt,ntd->nd/dot_general | solution.py:119
  317.0 5.3 %fusion.34 = f32[16,1,768]{2,1,0:T(1,128)S(1)} fusion(bf16[16,256,768]{2,1,0:T(8,128)(2,1)} %get-tuple-element.23, f32[16,256,1]{1,0,2:T(8,128)S(1)} %get-tuple-element.70), kind=kOutput, calls=%fused_computation.68 | convolution fusion | flops 37748736 | bytes 6356992 | tf_op jit(solution)/shard_map/nt,ntd->nd/dot_general | solution.py:119
  324.1 42.6 %shard_map.164 = (f32[16,16,768]{2,1,0:T(8,128)}, f32[16,16,192]{2,1,0:T(8,128)}, f32[16,16,768]{2,1,0:T(8,128)}, f32[16,16,192]{2,1,0:T(8,128)}) custom-call(f32[16,768]{1,0:T(8,128)} %bitcast_add_fusion.1.refs_0_, f32[16,192]{1,0:T(8,128)} %bitcast.157, f32[16,768]{1,0:T(8,128)} %bitcast_add_fusion.refs_2_, f32[16,192]{1,0:T(8,128)} %bitcast.156), custom_call_target="tpu_custom_call" | custom-call | tf_op jit(solution)/shard_map/pallas_call | solution.py:66
  366.7 2.9 fusion.45
  375.7 2.9 fusion.47
  383.9 2.8 copy.47
  388.4 3.0 multiply_reduce_fusion.1
  393.2 2.8 copy.50
  397.8 2.8 multiply_reduce_fusion
  401.2 8.7 %copy.26 = bf16[768,4096]{1,0:T(8,128)(2,1)} copy(bf16[768,4096]{0,1:T(8,128)(2,1)} %bitcast.125) | data formatting | bytes 12582912 | tf_op jit(solution)/shard_map/dot_general | solution.py:133
  410.0 5.5 %fusion.19.refs_1_ = f32[16,48,192]{2,1,0:T(8,128)} fusion(bf16[16,48,4096]{2,1,0:T(8,128)(2,1)} %bitcast.134, bf16[4096,192]{0,1:T(8,128)(2,1)S(1)} %copy-done.14), kind=kOutput, calls=%fused_computation.34 | convolution fusion | flops 1207959552 | bytes 8454144 | tf_op jit(solution)/shard_map/dot_general | solution.py:133
  415.5 8.7 %copy.24 = bf16[768,4096]{1,0:T(8,128)(2,1)} copy(bf16[768,4096]{0,1:T(8,128)(2,1)} %bitcast.124) | data formatting | bytes 12582912 | tf_op jit(solution)/shard_map/dot_general | solution.py:133
  424.2 5.5 %fusion.21.refs_0_ = f32[16,48,192]{2,1,0:T(8,128)} fusion(bf16[16,48,4096]{2,1,0:T(8,128)(2,1)} %bitcast.135, bf16[4096,192]{0,1:T(8,128)(2,1)S(1)} %copy-done.12), kind=kOutput, calls=%fused_computation.36 | convolution fusion | flops 1207959552 | bytes 8454144 | tf_op jit(solution)/shard_map/dot_general | solution.py:133
  429.7 35.8 %shard_map.165 = (f32[16,48,192]{2,1,0:T(8,128)}, f32[16,48,192]{2,1,0:T(8,128)}, f32[16,2,768]{2,1,0:T(2,128)}) custom-call(f32[16,48,192]{2,1,0:T(8,128)} %fusion.21.refs_0_, f32[16,48,192]{2,1,0:T(8,128)} %fusion.19.refs_1_, f32[2,768]{1,0:T(2,128)} %pad_maximum_fusion.refs_2_), custom_call_target="tpu_custom_call" | custom-call | tf_op jit(solution)/shard_map/pallas_call | solution.py:66
  470.7 36.1 %shard_map.166 = (f32[16,48,192]{2,1,0:T(8,128)}, f32[16,48,192]{2,1,0:T(8,128)}, f32[16,2,768]{2,1,0:T(2,128)}) custom-call(f32[48,192]{1,0:T(8,128)} %reduce_sum.186.refs_0_, f32[48,192]{1,0:T(8,128)} %reduce_sum.187.refs_1_, f32[2,768]{1,0:T(2,128)} %reduce_sum.188.refs_2_), custom_call_target="tpu_custom_call" | custom-call | tf_op jit(solution)/shard_map/pallas_call | solution.py:66
  506.8 2.2 copy.28
  (132 shorter events, 40.8 us)
Async XLA Ops:
  0.6 262.9 %copy-start = (bf16[768,192]{0,1:T(8,128)(2,1)S(1)}, bf16[768,192]{0,1:T(8,128)(2,1)}, u32[]{:S(2)}) copy-start(bf16[768,192]{0,1:T(8,128)(2,1)} %param.13) | copy-start | bytes 884740
  243.0 4.6 copy-start.2
  251.7 3.7 copy-start.20
  251.8 3.7 copy-start.17
  255.4 8.1 %copy-start.3 = (bf16[4096,768]{1,0:T(8,128)(2,1)}, bf16[4096,768]{1,0:T(8,128)(2,1)S(1)}, u32[]{:S(2)}) copy-start(bf16[4096,768]{1,0:T(8,128)(2,1)S(1)} %get-tuple-element.79) | copy-start | bytes 18874372
  258.0 4.6 copy-start.16
  263.5 4.1 copy-start.31
  267.6 4.1 copy-start.15
  317.0 53.2 %copy-start.32 = (s32[16,1,16]{2,1,0:T(1,128)S(1)}, s32[16,1,16]{2,1,0:T(1,128)}, u32[]{:S(2)}) copy-start(s32[16,1,16]{2,1,0:T(1,128)} %get-tuple-element.28) | copy-start | bytes 3076
  370.9 7.7 %copy-start.7 = (f32[256,256]{1,0:T(8,128)S(1)}, f32[256,256]{1,0:T(8,128)}, u32[]{:S(2)}) copy-start(f32[256,256]{1,0:T(8,128)} %get-tuple-element.77) | copy-start | bytes 786436
  370.9 7.7 %copy-start.10 = (f32[16,16,768]{2,1,0:T(8,128)S(1)}, f32[16,16,768]{2,1,0:T(8,128)}, u32[]{:S(2)}) copy-start(f32[16,16,768]{2,1,0:T(8,128)} %get-tuple-element.27) | copy-start | bytes 2359300
  370.9 9.5 %copy-start.19 = (f32[16,16,192]{2,1,0:T(8,128)S(1)}, f32[16,16,192]{2,1,0:T(8,128)}, u32[]{:S(2)}) copy-start(f32[16,16,192]{2,1,0:T(8,128)} %get-tuple-element.33) | copy-start | bytes 589828
  375.7 3.8 copy-start.8
  383.4 3.4 copy-start.6
  383.8 2.8 copy-start.27
  383.9 2.9 copy-start.29
  383.9 4.4 slice-start
  388.4 3.0 copy-start.11
  393.2 2.8 copy-start.26
  393.2 2.8 copy-start.28
  393.2 4.5 slice-start.2
  401.2 8.7 %copy-start.14 = (bf16[4096,192]{0,1:T(8,128)(2,1)S(1)}, bf16[4096,192]{0,1:T(8,128)(2,1)}, u32[]{:S(2)}) copy-start(bf16[4096,192]{0,1:T(8,128)(2,1)} %copy-done.13) | copy-start | bytes 4718596
  415.5 8.7 %copy-start.12 = (bf16[4096,192]{0,1:T(8,128)(2,1)S(1)}, bf16[4096,192]{0,1:T(8,128)(2,1)}, u32[]{:S(2)}) copy-start(bf16[4096,192]{0,1:T(8,128)(2,1)} %copy-done.11) | copy-start | bytes 4718596
  424.2 89.8 %copy-start.1 = (bf16[768,192]{0,1:T(8,128)(2,1)S(1)}, bf16[768,192]{0,1:T(8,128)(2,1)}, u32[]{:S(2)}) copy-start(bf16[768,192]{0,1:T(8,128)(2,1)} %param.13) | copy-start | bytes 884740
  (15 other events, 28.6 us)
